TPU v7x, 32 devices: a whole 2x2x4 slice. The times are simulated.
32 devices in a mesh: blk: 8 (over y, x, core), slab: 4 (over z).
Axes of the slice: x: 2, y: 2, z: 4, core: 2. Of those that a mesh axis runs over, the one named last changes fastest.
Arguments:
- old_factor: bfloat16 [8192, 24576], P('slab', 'blk'), may hold values from -0.0546875 to 0.0546875
- solved: bfloat16 [24576, 256], P('blk', 'slab'), may hold values from -6 to 6
- band: bfloat16 [8192, 8192], P('blk'), may hold values from -0.0625 to 0.0625
- inv_diag: bfloat16 [2048, 8192], P(None, 'blk'), may hold values from -1 to 2, as said below
- rhs: bfloat16 [8192, 256], P('blk', 'slab'), may hold values from -6 to 6
Outputs:
- solution: bfloat16 [8192, 256], P('blk', 'slab')
Inputs may be any that keep to these rules, and one draw needn't show every extreme that they name: `inv_diag`: columns k * 2048 to (k + 1) * 2048 - 1 hold the inverse applied in block step k.
All inputs are finite; a program needn't handle non-finite values.
Results may differ from a plain program's by a relative error of at most 0.008.
Values may be sent and summed in bfloat16 or wider, within the bound.
A program may use at most 64 MiB of HBM per device.

v0:
```python
import jax
import jax.numpy as jnp
from jax import lax
from jax.sharding import PartitionSpec as P

STEPS = 4


def body(old_factor, solved, band, inv_diag, rhs):
    own_rows = rhs.shape[0]
    block_rows = inv_diag.shape[0]
    group_size = block_rows // own_rows
    own_index = lax.axis_index("blk")
    own_block = own_index // group_size
    offset = own_index % group_size * own_rows
    partial_value = jnp.dot(
        old_factor,
        lax.all_gather(solved, "slab", axis=1, tiled=True),
        preferred_element_type=jnp.float32,
    )
    window_terms = lax.all_to_all(partial_value, "slab", split_axis=1, concat_axis=0, tiled=True)
    source = rhs.astype(jnp.float32)
    accum = lax.psum_scatter(window_terms, "blk", scatter_dimension=0, tiled=True)
    solution = jnp.zeros(rhs.shape, jnp.bfloat16)
    for step in range(STEPS):
        total = accum
        resid = (source - total).astype(jnp.bfloat16)
        term = jnp.dot(inv_diag, resid, preferred_element_type=jnp.float32)
        term = jnp.where(own_block == step, term, jnp.zeros_like(term))
        newest = lax.psum(term, "blk").astype(jnp.bfloat16)
        mine = lax.dynamic_slice_in_dim(newest, offset, own_rows, 0)
        solution = jnp.where(own_block == step, mine, solution)
        if step + 1 < STEPS:
            columns = band[:, step * block_rows : (step + 1) * block_rows]
            update = jnp.dot(columns, newest, preferred_element_type=jnp.float32)
            accum = accum + jnp.where(own_block > step, update, jnp.zeros_like(update))
    return solution


def solution(mesh):
    return jax.shard_map(
        body,
        mesh=mesh,
        in_specs=(
            P("slab", "blk"),
            P("blk", "slab"),
            P("blk", None),
            P(None, "blk"),
            P("blk", "slab"),
        ),
        out_specs=P("blk", "slab"),
        check_vma=False,
    )
```

profile of v0, /device:TPU:0, one launch (start us, length us, event | category | flops | bytes accessed | tf_op | source)
XLA Modules:
  0.0 292.5 jit_solution(17000383142873836997)
XLA Ops:
  6.5 0.0 all-gather.2.cloned.1.call-start
  6.5 0.7 all-gather.2.cloned.1.call-update
  7.3 0.0 reduce-scatter.2.cloned.1.call-start
  7.3 41.4 %all-gather.2.cloned.1.call-done = bf16[3072,256]{0,1:T(8,128)(2,1)} async-done(((bf16[3072,64]{0,1:T(8,128)(2,1)}), bf16[3072,256]{0,1:T(8,128)(2,1)}) %all-gather.2.cloned.1.call-update) | async-done | bytes 1572880 | tf_op jit(solution)/shard_map/all_gather | solution.py:18
  48.7 6.9 %fusion.56 = f32[2048,256]{0,1:T(8,128)S(1)} fusion(bf16[2048,3072]{1,0:T(8,128)(2,1)} %param.5, bf16[3072,256]{0,1:T(8,128)(2,1)} %all-gather.2.cloned.1.call-done), kind=kOutput, calls=%fused_computation.37 | convolution fusion | flops 3221225472 | bytes 16252928 | tf_op jit(solution)/shard_map/dot_general | solution.py:16
  55.6 50.4 %all_to_all.19 = f32[2048,4,64]{0,2,1:T(8,128)S(1)} all-to-all(f32[2048,4,64]{0,2,1:T(8,128)S(1)} %bitcast.41), channel_id=1, replica_groups=mesh['blk'=8,'slab'=4] {'slab'}, dimensions={1} | all-to-all | bytes 4194304 | tf_op jit(solution)/shard_map/all_to_all | solution.py:21
  106.0 0.0 copy-start.2
  106.0 1.5 copy.7
  107.5 0.0 reduce-scatter.2.cloned.1.call-update
  107.6 40.6 %reduce-scatter.2.cloned.1.call-done = f32[1024,64]{0,1:T(8,128)} async-done(((f32[8192,64]{0,1:T(8,128)}), f32[1024,64]{0,1:T(8,128)}) %reduce-scatter.2.cloned.1.call-update) | async-done | bytes 262160 | tf_op jit(solution)/shard_map/reduce_scatter | solution.py:23
  148.2 0.0 copy-done.2
  148.2 0.0 copy-start.3
  148.2 3.7 %fusion.6 = f32[2048,64]{0,1:T(8,128)S(1)} fusion(bf16[2048,1024]{1,0:T(8,128)(2,1)} %param.8, pred[]{:T(512)S(6)} %eq.19, f32[1024,64]{0,1:T(8,128)} %reduce-scatter.2.cloned.1.call-done, bf16[1024,64]{0,1:T(8,128)(2,1)S(1)} %copy-done.2), kind=kOutput, calls=%fused_computation.10 | convolution fusion | flops 268763136 | bytes 5111809 | tf_op jit(solution)/shard_map/dot_general | solution.py:28
  151.9 29.6 %all-reduce.4 = bf16[2048,64]{0,1:T(8,128)(2,1)S(1)} all-reduce(f32[2048,64]{0,1:T(8,128)S(1)} %fusion.6), channel_id=1, replica_groups=mesh['blk'=8,'slab'=4] {'blk'}, use_global_device_ids=true, to_apply=%region_1.2 | all-reduce | flops 131072 | bytes 786432 | tf_op jit(solution)/shard_map/psum | solution.py:30
  181.5 0.0 copy-done.3
  181.5 0.0 copy-start
  181.5 3.7 %fusion.16 = f32[1024,64]{0,1:T(8,128)S(1)} fusion(f32[1024,64]{0,1:T(8,128)S(1)} %copy-done.3, bf16[2048,64]{0,1:T(8,128)(2,1)S(1)} %all-reduce.4, bf16[1024,8192]{1,0:T(8,128)(2,1)} %param.7, pred[]{:T(512)S(6)} %gt.9), kind=kOutput, calls=%fused_computation.16 | convolution fusion | flops 268566528 | bytes 4980737 | tf_op jit(solution)/shard_map/dot_general | solution.py:35
  185.3 0.0 copy-done
  185.3 1.4 fusion.7
  186.7 29.4 %all-reduce.5 = bf16[2048,64]{0,1:T(8,128)(2,1)S(1)} all-reduce(f32[2048,64]{0,1:T(8,128)S(1)} %fusion.7), channel_id=1, replica_groups=mesh['blk'=8,'slab'=4] {'blk'}, use_global_device_ids=true, to_apply=%region_2.3 | all-reduce | flops 131072 | bytes 786432 | tf_op jit(solution)/shard_map/psum | solution.py:30
  216.1 0.0 copy-start.1
  216.1 3.7 %fusion.25 = f32[1024,64]{0,1:T(8,128)S(1)} fusion(f32[1024,64]{0,1:T(8,128)S(1)} %fusion.16, bf16[2048,64]{0,1:T(8,128)(2,1)S(1)} %all-reduce.5, bf16[1024,8192]{1,0:T(8,128)(2,1)} %param.7, pred[]{:T(512)S(6)} %gt.10), kind=kOutput, calls=%fused_computation.19 | convolution fusion | flops 268566528 | bytes 4980737 | tf_op jit(solution)/shard_map/dot_general | solution.py:35
  219.8 0.0 copy-done.1
  219.8 1.4 fusion.8
  221.2 28.8 %all-reduce.6 = bf16[2048,64]{0,1:T(8,128)(2,1)S(1)} all-reduce(f32[2048,64]{0,1:T(8,128)S(1)} %fusion.8), channel_id=1, replica_groups=mesh['blk'=8,'slab'=4] {'blk'}, use_global_device_ids=true, to_apply=%region_3.4 | all-reduce | flops 131072 | bytes 786432 | tf_op jit(solution)/shard_map/psum | solution.py:30
  250.0 6.2 %fusion.9 = f32[2048,64]{0,1:T(8,128)S(1)} fusion(bf16[2048,1024]{1,0:T(8,128)(2,1)} %param.8, f32[1024,64]{0,1:T(8,128)S(1)} %fusion.25, bf16[2048,64]{0,1:T(8,128)(2,1)S(1)} %all-reduce.6, bf16[1024,8192]{1,0:T(8,128)(2,1)} %param.7, bf16[1024,64]{0,1:T(8,128)(2,1)S(1)} %copy-done.2, pred[]{:T(512)S(6)} %eq.18, pred[]{:T(512)S(6)} %gt.11), kind=kOutput, calls=%fused_computation.13 | convolution fusion | flops 537329664 | bytes 9568258 | tf_op jit(solution)/shard_map/dot_general | solution.py:28
  256.2 28.8 %all-reduce.7 = bf16[2048,64]{0,1:T(8,128)(2,1)S(1)} all-reduce(f32[2048,64]{0,1:T(8,128)S(1)} %fusion.9), channel_id=1, replica_groups=mesh['blk'=8,'slab'=4] {'blk'}, use_global_device_ids=true, to_apply=%region_4.5 | all-reduce | flops 131072 | bytes 786432 | tf_op jit(solution)/shard_map/psum | solution.py:30
  284.9 0.7 fusion.49
Async XLA Ops:
  6.5 42.1 %all-gather.2.cloned.1.call-start = ((), (), s32[]{:S(2)}) async-start(), calls=%async_computation.2 | async-start | bytes 1966080 | tf_op jit(solution)/shard_map/all_gather | solution.py:18
  7.3 140.9 %reduce-scatter.2.cloned.1.call-start = ((), (), s32[]{:S(2)}) async-start(), calls=%async_computation.3 | async-start | bytes 2359296 | tf_op jit(solution)/shard_map/reduce_scatter | solution.py:23
  106.0 42.2 %copy-start.2 = (bf16[1024,64]{0,1:T(8,128)(2,1)S(1)}, bf16[1024,64]{0,1:T(8,128)(2,1)}, u32[]{:S(2)}) copy-start(bf16[1024,64]{0,1:T(8,128)(2,1)} %param.9) | copy-start | bytes 393220
  148.2 33.3 %copy-start.3 = (f32[1024,64]{0,1:T(8,128)S(1)}, f32[1024,64]{0,1:T(8,128)}, u32[]{:S(2)}) copy-start(f32[1024,64]{0,1:T(8,128)} %reduce-scatter.2.cloned.1.call-done) | copy-start | bytes 786436
  181.5 3.7 %copy-start = (bf16[2048,1024]{1,0:T(8,128)(2,1)S(1)}, bf16[2048,1024]{1,0:T(8,128)(2,1)}, u32[]{:S(2)}) copy-start(bf16[2048,1024]{1,0:T(8,128)(2,1)} %param.8) | copy-start | bytes 12582916
  216.1 3.7 %copy-start.1 = (bf16[2048,1024]{1,0:T(8,128)(2,1)S(1)}, bf16[2048,1024]{1,0:T(8,128)(2,1)}, u32[]{:S(2)}) copy-start(bf16[2048,1024]{1,0:T(8,128)(2,1)} %param.8) | copy-start | bytes 12582916
Sparse Core Ops, SparseCore 0:
  8.9 39.7 all-gather.1
  107.7 40.4 reduce-scatter.1
where the time goes:
time: 293 us
  blocking collectives  167 us (57%)
  waiting for transfers between devices  82.7 us (28%)
  matrix products  27 us (9%)
  between operations  13.5 us (5%)
    psum x4, blocking collectives, body(): newest = lax.psum(term, 'blk').astype(jnp.bfloat16)  117 us
    all_to_all x1, blocking collectives, body(): lax.all_to_all(partial_value, 'slab', split_axis=1, concat_axis=0, tiled=...  50.4 us
    all_gather x1, waiting for transfers between devices, body(): lax.all_gather(solved, 'slab', axis=1, tiled=True)  41.4 us
    reduce_scatter x1, waiting for transfers between devices, body(): lax.psum_scatter(window_terms, 'blk', scatter_dimension=0, tiled=True)  40.6 us
    dot_general x4, matrix products, body(): term = jnp.dot(inv_diag, resid, preferred_element_type=jnp.float32)  12.6 us
    dot_general x2, matrix products, body(): update = jnp.dot(columns, newest, preferred_element_type=jnp.float32)  7.47 us
    dot_general x1, matrix products, body(): jnp.dot(old_factor, lax.all_gather(solved, 'slab', axis=1, tiled=True), p...  6.89 us
  transfers between devices with their start and end apart: 2, of which 2 were waited for; matrix products, arithmetic and copies ran while one was open for 0% of the time, Pallas kernels for 0%

commit v1 on v0

--- a/solution.py
+++ b/solution.py
@@ -4,6 +4,28 @@
 from jax.sharding import PartitionSpec as P
 
 STEPS = 4
+
+
+def in_order(blocks, dim):
+    blocks = jnp.moveaxis(blocks, 0, dim)
+    dims = blocks.shape
+    return blocks.reshape(*dims[:dim], dims[dim] * dims[dim + 1], *dims[dim + 2 :])
+
+
+def ring_gather(shard, axis, dim):
+    size = lax.axis_size(axis)
+    pairs = [(i, (i + 1) % size) for i in range(size)]
+    back = [(b, a) for a, b in pairs]
+    lower, upper = ([], [])
+    for turn in range(size - 1):
+        if turn % 2 == 0:
+            lower.append(lax.ppermute(lower[-1] if lower else shard, axis, pairs))
+        else:
+            upper.append(lax.ppermute(upper[-1] if upper else shard, axis, back))
+    tiles = jnp.stack([*lower[::-1], shard, *upper])
+    shift = lax.axis_index(axis) - len(lower)
+    tiles = tiles[(jnp.arange(size) - shift) % size]
+    return in_order(tiles, dim)
 
 
 def body(old_factor, solved, band, inv_diag, rhs):
@@ -14,9 +36,7 @@
     own_block = own_index // group_size
     offset = own_index % group_size * own_rows
     partial_value = jnp.dot(
-        old_factor,
-        lax.all_gather(solved, "slab", axis=1, tiled=True),
-        preferred_element_type=jnp.float32,
+        old_factor, ring_gather(solved, "slab", 1), preferred_element_type=jnp.float32
     )
     window_terms = lax.all_to_all(partial_value, "slab", split_axis=1, concat_axis=0, tiled=True)
     source = rhs.astype(jnp.float32)

time: 293 us -> 281 us (0.959)
  waiting for transfers between devices: 82.7 us -> 66.5 us
  starting transfers between devices: 0.04 us -> 5.08 us
    all_gather x1 -> x0, waiting for transfers between devices: 41.4 us -> none  [body(): lax.all_gather(solved, 'slab', axis=1, tiled=True)]
    ppermute x0 -> x3, waiting for transfers between devices: none -> 26.2 us  [the longest x2 19 us: ring_gather(): lower.append(lax.ppermute(lower[-1] if lower else shard, axis, pairs))]
    ppermute x0 -> x3, starting transfers between devices: none -> 5.08 us  [the longest x2 3.05 us: ring_gather(): lower.append(lax.ppermute(lower[-1] if lower else shard, axis, pairs))]
  transfers between devices with their start and end apart: 2 -> 4, of which waited for: 2 -> 4; matrix products, arithmetic and copies ran while one was open for 0% -> 0% of each run, Pallas kernels for 0% -> 0%
where the time goes in v1:
time: 281 us
  blocking collectives  165 us (59%)
  waiting for transfers between devices  66.5 us (24%)
  matrix products  26.6 us (9%)
  between operations  13.5 us (5%)
  starting transfers between devices  5.08 us (2%)
    psum x4, blocking collectives, body(): newest = lax.psum(term, 'blk').astype(jnp.bfloat16)  116 us
    all_to_all x1, blocking collectives, body(): lax.all_to_all(partial_value, 'slab', split_axis=1, concat_axis=0, tiled=...  48.7 us
    reduce_scatter x1, waiting for transfers between devices, body(): lax.psum_scatter(window_terms, 'blk', scatter_dimension=0, tiled=True)  40.3 us
    ppermute x2, waiting for transfers between devices, ring_gather(): lower.append(lax.ppermute(lower[-1] if lower else shard, axis, pairs))  19 us
    dot_general x4, matrix products, body(): term = jnp.dot(inv_diag, resid, preferred_element_type=jnp.float32)  12.6 us
    dot_general x2, matrix products, body(): update = jnp.dot(columns, newest, preferred_element_type=jnp.float32)  7.47 us
    ppermute x1, waiting for transfers between devices, ring_gather(): upper.append(lax.ppermute(upper[-1] if upper else shard, axis, back))  7.18 us
    dot_general x1, matrix products, body(): jnp.dot(old_factor, ring_gather(solved, 'slab', 1), preferred_element_typ...  6.47 us
  transfers between devices with their start and end apart: 4, of which 4 were waited for; matrix products, arithmetic and copies ran while one was open for 0% of the time, Pallas kernels for 0%

profile of v1, /device:TPU:0, one launch (start us, length us, event | category | flops | bytes accessed | tf_op | source)
XLA Modules:
  0.0 281.0 jit_solution(1706611519335076434)
XLA Ops:
  6.5 0.0 reduce-scatter.2.cloned.1.call-start
  6.5 3.1 %collective-permute-start = (bf16[3072,64]{0,1:T(8,128)(2,1)}, bf16[3072,64]{0,1:T(8,128)(2,1)S(1)}, u32[]{:S(2)}, u32[]{:S(2)}) collective-permute-start(bf16[3072,64]{0,1:T(8,128)(2,1)} %param.6), channel_id=1, source_target_pairs={{0,1},{1,2},{2,3},{3,0},{4,5},{5,6},{6,7},{7,4},{8,9},{9,10},{10,1... | collective-permute-start | bytes 1179656 | tf_op jit(solution)/shard_map/ppermute | solution.py:22
  9.6 2.0 collective-permute-start.2
  11.6 10.2 %collective-permute-done = bf16[3072,64]{0,1:T(8,128)(2,1)S(1)} collective-permute-done((bf16[3072,64]{0,1:T(8,128)(2,1)}, bf16[3072,64]{0,1:T(8,128)(2,1)S(1)}, u32[]{:S(2)}, u32[]{:S(2)}) %collective-permute-start) | collective-permute-done | bytes 393248 | tf_op jit(solution)/shard_map/ppermute | solution.py:22
  21.8 0.0 collective-permute-start.1
  21.9 7.2 %collective-permute-done.2 = bf16[3072,64]{0,1:T(8,128)(2,1)S(1)} collective-permute-done((bf16[3072,64]{0,1:T(8,128)(2,1)}, bf16[3072,64]{0,1:T(8,128)(2,1)S(1)}, u32[]{:S(2)}, u32[]{:S(2)}) %collective-permute-start.2) | collective-permute-done | bytes 393248 | tf_op jit(solution)/shard_map/ppermute | solution.py:24
  29.0 8.8 %collective-permute-done.1 = bf16[3072,64]{0,1:T(8,128)(2,1)S(1)} collective-permute-done((bf16[3072,64]{0,1:T(8,128)(2,1)S(1)}, bf16[3072,64]{0,1:T(8,128)(2,1)S(1)}, u32[]{:S(2)}, u32[]{:S(2)}) %collective-permute-start.1) | collective-permute-done | bytes 393248 | tf_op jit(solution)/shard_map/ppermute | solution.py:22
  37.8 1.2 pad_maximum_fusion
  39.0 0.6 gather_fusion
  39.7 6.5 %fusion.58 = f32[256,2048]{1,0:T(8,128)S(1)} fusion(bf16[3072,256]{0,1:T(8,128)(2,1)S(1)} %bitcast.52, bf16[2048,3072]{1,0:T(8,128)(2,1)} %param.5), kind=kOutput, calls=%fused_computation.46 | convolution fusion | flops 3221225472 | bytes 16252928 | tf_op jit(solution)/shard_map/dot_general | solution.py:38
  46.2 48.7 %all_to_all.19 = f32[2048,4,64]{0,2,1:T(8,128)S(1)} all-to-all(f32[2048,4,64]{0,2,1:T(8,128)S(1)} %bitcast.53), channel_id=1, replica_groups=mesh['blk'=8,'slab'=4] {'slab'}, dimensions={1} | all-to-all | bytes 4194304 | tf_op jit(solution)/shard_map/all_to_all | solution.py:41
  94.9 0.0 copy-start.2
  94.9 1.5 copy.7
  96.4 0.0 reduce-scatter.2.cloned.1.call-update
  96.4 40.3 %reduce-scatter.2.cloned.1.call-done = f32[1024,64]{0,1:T(8,128)} async-done(((f32[8192,64]{0,1:T(8,128)}), f32[1024,64]{0,1:T(8,128)}) %reduce-scatter.2.cloned.1.call-update) | async-done | bytes 262160 | tf_op jit(solution)/shard_map/reduce_scatter | solution.py:43
  136.7 0.0 copy-done.2
  136.7 0.0 copy-start.3
  136.7 3.7 %fusion.6 = f32[2048,64]{0,1:T(8,128)S(1)} fusion(bf16[2048,1024]{1,0:T(8,128)(2,1)} %param.8, pred[]{:T(512)S(6)} %eq.21, f32[1024,64]{0,1:T(8,128)} %reduce-scatter.2.cloned.1.call-done, bf16[1024,64]{0,1:T(8,128)(2,1)S(1)} %copy-done.2), kind=kOutput, calls=%fused_computation.11 | convolution fusion | flops 268763136 | bytes 5111809 | tf_op jit(solution)/shard_map/dot_general | solution.py:48
  140.4 29.6 %all-reduce.4 = bf16[2048,64]{0,1:T(8,128)(2,1)S(1)} all-reduce(f32[2048,64]{0,1:T(8,128)S(1)} %fusion.6), channel_id=1, replica_groups=mesh['blk'=8,'slab'=4] {'blk'}, use_global_device_ids=true, to_apply=%region_1.2 | all-reduce | flops 131072 | bytes 786432 | tf_op jit(solution)/shard_map/psum | solution.py:50
  170.1 0.0 copy-done.3
  170.1 0.0 copy-start
  170.1 3.7 %fusion.16 = f32[1024,64]{0,1:T(8,128)S(1)} fusion(f32[1024,64]{0,1:T(8,128)S(1)} %copy-done.3, bf16[2048,64]{0,1:T(8,128)(2,1)S(1)} %all-reduce.4, bf16[1024,8192]{1,0:T(8,128)(2,1)} %param.7, pred[]{:T(512)S(6)} %gt.9), kind=kOutput, calls=%fused_computation.18 | convolution fusion | flops 268566528 | bytes 4980737 | tf_op jit(solution)/shard_map/dot_general | solution.py:55
  173.9 0.0 copy-done
  173.9 1.4 fusion.7
  175.3 29.2 %all-reduce.5 = bf16[2048,64]{0,1:T(8,128)(2,1)S(1)} all-reduce(f32[2048,64]{0,1:T(8,128)S(1)} %fusion.7), channel_id=1, replica_groups=mesh['blk'=8,'slab'=4] {'blk'}, use_global_device_ids=true, to_apply=%region_2.3 | all-reduce | flops 131072 | bytes 786432 | tf_op jit(solution)/shard_map/psum | solution.py:50
  204.5 0.0 copy-start.1
  204.5 3.7 %fusion.25 = f32[1024,64]{0,1:T(8,128)S(1)} fusion(f32[1024,64]{0,1:T(8,128)S(1)} %fusion.16, bf16[2048,64]{0,1:T(8,128)(2,1)S(1)} %all-reduce.5, bf16[1024,8192]{1,0:T(8,128)(2,1)} %param.7, pred[]{:T(512)S(6)} %gt.10), kind=kOutput, calls=%fused_computation.21 | convolution fusion | flops 268566528 | bytes 4980737 | tf_op jit(solution)/shard_map/dot_general | solution.py:55
  208.3 0.0 copy-done.1
  208.3 1.4 fusion.8
  209.7 28.8 %all-reduce.6 = bf16[2048,64]{0,1:T(8,128)(2,1)S(1)} all-reduce(f32[2048,64]{0,1:T(8,128)S(1)} %fusion.8), channel_id=1, replica_groups=mesh['blk'=8,'slab'=4] {'blk'}, use_global_device_ids=true, to_apply=%region_3.4 | all-reduce | flops 131072 | bytes 786432 | tf_op jit(solution)/shard_map/psum | solution.py:50
  238.4 6.2 %fusion.9 = f32[2048,64]{0,1:T(8,128)S(1)} fusion(bf16[2048,1024]{1,0:T(8,128)(2,1)} %param.8, f32[1024,64]{0,1:T(8,128)S(1)} %fusion.25, bf16[2048,64]{0,1:T(8,128)(2,1)S(1)} %all-reduce.6, bf16[1024,8192]{1,0:T(8,128)(2,1)} %param.7, bf16[1024,64]{0,1:T(8,128)(2,1)S(1)} %copy-done.2, pred[]{:T(512)S(6)} %eq.20, pred[]{:T(512)S(6)} %gt.11), kind=kOutput, calls=%fused_computation.14 | convolution fusion | flops 537329664 | bytes 9568258 | tf_op jit(solution)/shard_map/dot_general | solution.py:48
  244.6 28.8 %all-reduce.7 = bf16[2048,64]{0,1:T(8,128)(2,1)S(1)} all-reduce(f32[2048,64]{0,1:T(8,128)S(1)} %fusion.9), channel_id=1, replica_groups=mesh['blk'=8,'slab'=4] {'blk'}, use_global_device_ids=true, to_apply=%region_4.5 | all-reduce | flops 131072 | bytes 786432 | tf_op jit(solution)/shard_map/psum | solution.py:50
  273.4 0.7 fusion.49
  (2 shorter events, 0.0 us)
Async XLA Ops:
  6.5 130.2 %reduce-scatter.2.cloned.1.call-start = ((), (), s32[]{:S(2)}) async-start(), calls=%async_computation.2 | async-start | bytes 2359296 | tf_op jit(solution)/shard_map/reduce_scatter | solution.py:43
  6.5 15.3 %collective-permute-start = (bf16[3072,64]{0,1:T(8,128)(2,1)}, bf16[3072,64]{0,1:T(8,128)(2,1)S(1)}, u32[]{:S(2)}, u32[]{:S(2)}) collective-permute-start(bf16[3072,64]{0,1:T(8,128)(2,1)} %param.6), channel_id=1, source_target_pairs={{0,1},{1,2},{2,3},{3,0},{4,5},{5,6},{6,7},{7,4},{8,9},{9,10},{10,1... | collective-permute-start | bytes 1179656 | tf_op jit(solution)/shard_map/ppermute | solution.py:22
  9.6 19.5 %collective-permute-start.2 = (bf16[3072,64]{0,1:T(8,128)(2,1)}, bf16[3072,64]{0,1:T(8,128)(2,1)S(1)}, u32[]{:S(2)}, u32[]{:S(2)}) collective-permute-start(bf16[3072,64]{0,1:T(8,128)(2,1)} %param.6), channel_id=1, source_target_pairs={{1,0},{2,1},{3,2},{0,3},{5,4},{6,5},{7,6},{4,7},{9,8},{10,9},{11,1... | collective-permute-start | bytes 1179656 | tf_op jit(solution)/shard_map/ppermute | solution.py:24
  21.8 16.0 %collective-permute-start.1 = (bf16[3072,64]{0,1:T(8,128)(2,1)S(1)}, bf16[3072,64]{0,1:T(8,128)(2,1)S(1)}, u32[]{:S(2)}, u32[]{:S(2)}) collective-permute-start(bf16[3072,64]{0,1:T(8,128)(2,1)S(1)} %collective-permute-done), channel_id=1, source_target_pairs={{0,1},{1,2},{2,3},{3,0},{4,5},{5,6},{6,7},{7,4},{8,9},{9,10},{10,1... | collective-permute-start | bytes 1179656 | tf_op jit(solution)/shard_map/ppermute | solution.py:22
  94.9 41.9 %copy-start.2 = (bf16[1024,64]{0,1:T(8,128)(2,1)S(1)}, bf16[1024,64]{0,1:T(8,128)(2,1)}, u32[]{:S(2)}) copy-start(bf16[1024,64]{0,1:T(8,128)(2,1)} %param.9) | copy-start | bytes 393220
  136.7 33.4 %copy-start.3 = (f32[1024,64]{0,1:T(8,128)S(1)}, f32[1024,64]{0,1:T(8,128)}, u32[]{:S(2)}) copy-start(f32[1024,64]{0,1:T(8,128)} %reduce-scatter.2.cloned.1.call-done) | copy-start | bytes 786436
  170.1 3.8 %copy-start = (bf16[2048,1024]{1,0:T(8,128)(2,1)S(1)}, bf16[2048,1024]{1,0:T(8,128)(2,1)}, u32[]{:S(2)}) copy-start(bf16[2048,1024]{1,0:T(8,128)(2,1)} %param.8) | copy-start | bytes 12582916
  204.5 3.8 %copy-start.1 = (bf16[2048,1024]{1,0:T(8,128)(2,1)S(1)}, bf16[2048,1024]{1,0:T(8,128)(2,1)}, u32[]{:S(2)}) copy-start(bf16[2048,1024]{1,0:T(8,128)(2,1)} %param.8) | copy-start | bytes 12582916
Sparse Core Ops, SparseCore 0:
  96.5 40.1 reduce-scatter.1
